TPU v7x, 512 devices: a whole 4x8x8 slice. The times are simulated.
512 devices in a mesh: traj: 8 (over z), dom: 64 (over x, y, core).
Axes of the slice: x: 4, y: 8, z: 8, core: 2. Of those that a mesh axis runs over, the one named last changes fastest.
Arguments:
- node_lat: bfloat16 [8, 16384, 512], P('traj', 'dom'), may hold values from -6 to 6
- edge_lat: bfloat16 [8, 32768, 512], P('traj', 'dom'), may hold values from -6 to 6
- grad_edge: bfloat16 [8, 32768, 512], P('traj', 'dom'), may hold values from -6 to 6
- grad_agg: bfloat16 [8, 16384, 512], P('traj', 'dom'), may hold values from -6 to 6
- weight_edge: bfloat16 [512, 512], replicated, may hold values from -0.15625 to 0.15625
- weight_send: bfloat16 [512, 512], replicated, may hold values from -0.15625 to 0.15625
- weight_recv: bfloat16 [512, 512], replicated, may hold values from -0.15625 to 0.15625
- weight_out: bfloat16 [512, 512], replicated, may hold values from -0.25 to 0.25
- edge_src: int32 [32768], P('dom'), may hold values from 0 to 767
- edge_recv_block: int32 [256], P('dom'), may hold values from 0 to 1
- edge_recv_node: int32 [32768], P('dom'), may hold values from 0 to 127
- send_blocks: int32 [256], P('dom'), may hold values from 0 to 1
Outputs:
- agg: bfloat16 [8, 16384, 512], P('traj', 'dom')
- grad_edge_lat: bfloat16 [8, 32768, 512], P('traj', 'dom')
- grad_node_lat: bfloat16 [8, 16384, 512], P('traj', 'dom')
- weight_grads: float32 [4, 512, 512], P(None, 'dom')
Inputs may be any that keep to these rules, and one draw needn't show every extreme that they name: edge_src // 128 is a slot below 6.
All inputs are finite; a program needn't handle non-finite values.
Results may differ from a plain program's by a relative error of at most 0.012.
Values may be sent and summed in bfloat16 or wider, within the bound.
A program may use at most 64 MiB of HBM per device.

v0:
```python
import jax
import jax.numpy as jnp
from jax import lax
from jax.sharding import PartitionSpec as P

ROUNDS = 4


def partner(shard, axis, stride):
    return lax.ppermute(shard, axis, [(i, i ^ 1 << stride) for i in range(lax.axis_size(axis))])


def dot_rows(former, latter):
    return lax.dot_general(
        former, latter, (((0,), (0,)), ((), ())), preferred_element_type=jnp.float32
    )


def dot_cols(former, latter):
    return lax.dot_general(
        former, latter, (((1,), (1,)), ((), ())), preferred_element_type=jnp.float32
    )


def dot_cols_exact(former, latter):
    return lax.dot_general(
        former,
        latter.astype(jnp.float32),
        (((1,), (1,)), ((), ())),
        precision=lax.Precision.HIGHEST,
        preferred_element_type=jnp.float32,
    )


def silu_grad(preact):
    sigmoid_val = jax.nn.sigmoid(preact)
    return sigmoid_val * (1.0 + preact * (1.0 - sigmoid_val))


def per_device(
    node_lat,
    edge_lat,
    grad_edge,
    grad_agg,
    weight_edge,
    weight_send,
    weight_recv,
    weight_out,
    edge_src,
    edge_recv_block,
    edge_recv_node,
    send_blocks,
):
    features = node_lat.shape[2]
    node_rows = node_lat[0]
    node_count = node_rows.shape[0]
    block_count = node_count // 128
    edge_rows = edge_lat[0]
    edge_count = edge_rows.shape[0]
    node_blocks = node_rows.reshape(block_count, 128, features)
    block_pick = (send_blocks[:, None] == jnp.arange(block_count, dtype=jnp.int32)[None, :]).astype(
        jnp.bfloat16
    )
    outgoing = jnp.einsum(
        "rb,bnd->rnd", block_pick, node_blocks, preferred_element_type=jnp.float32
    ).astype(jnp.bfloat16)
    received = []
    for section in range(ROUNDS):
        received.append(partner(outgoing[section], "dom", section))
    node_table = jnp.concatenate([node_rows] + received, axis=0)
    slot_count = node_table.shape[0]
    receiver = (
        jnp.repeat(edge_recv_block, 128, total_repeat_length=edge_count) * 128 + edge_recv_node
    )
    onehot_src = (edge_src[:, None] == jnp.arange(slot_count, dtype=jnp.int32)[None, :]).astype(
        jnp.bfloat16
    )
    onehot_recv = (receiver[:, None] == jnp.arange(node_count, dtype=jnp.int32)[None, :]).astype(
        jnp.bfloat16
    )
    send_rows = jnp.dot(onehot_src, node_table, preferred_element_type=jnp.float32).astype(
        jnp.bfloat16
    )
    recv_rows = jnp.dot(onehot_recv, node_rows, preferred_element_type=jnp.float32).astype(
        jnp.bfloat16
    )
    preact = jnp.dot(edge_rows, weight_edge, preferred_element_type=jnp.float32)
    preact = preact + jnp.dot(send_rows, weight_send, preferred_element_type=jnp.float32)
    preact = preact + jnp.dot(recv_rows, weight_recv, preferred_element_type=jnp.float32)
    hidden = jax.nn.silu(preact).astype(jnp.bfloat16)
    projected = jnp.dot(hidden, weight_out, preferred_element_type=jnp.float32)
    centered = projected - jnp.mean(projected, axis=1, keepdims=True)
    inv_std = lax.rsqrt(jnp.mean(centered * centered, axis=1, keepdims=True) + 1e-05)
    normed = centered * inv_std
    message = normed.astype(jnp.bfloat16)
    agg = dot_rows(onehot_recv, message)
    grad_msg = grad_edge[0].astype(jnp.float32) + jnp.dot(
        onehot_recv, grad_agg[0], preferred_element_type=jnp.float32
    )
    grad_proj = inv_std * (
        grad_msg
        - jnp.mean(grad_msg, axis=1, keepdims=True)
        - normed * jnp.mean(grad_msg * normed, axis=1, keepdims=True)
    )
    grad_proj = grad_proj.astype(jnp.bfloat16)
    grad_preact = (dot_cols(grad_proj, weight_out) * silu_grad(preact)).astype(jnp.bfloat16)
    partial_grads = jnp.stack(
        [
            dot_rows(edge_rows, grad_preact),
            dot_rows(send_rows, grad_preact),
            dot_rows(recv_rows, grad_preact),
            dot_rows(hidden, grad_proj),
        ]
    )
    grad_edges = grad_edge[0].astype(jnp.float32) + dot_cols(grad_preact, weight_edge)
    slot_sums = dot_rows(onehot_src, grad_preact)
    recv_sums = dot_rows(onehot_recv, grad_preact)
    slot_grads = dot_cols_exact(slot_sums, weight_send)
    local_grads = slot_grads[:node_count] + dot_cols_exact(recv_sums, weight_recv)
    local_blocks = local_grads.reshape(block_count, 128, features)
    borrowed = slot_grads[node_count:].reshape(ROUNDS, 128, features)
    returned_list = []
    for section in range(ROUNDS):
        returned_list.append(
            partner(borrowed[section].astype(jnp.bfloat16), "dom", section).astype(jnp.float32)
        )
    returned = jnp.stack(returned_list)
    local_blocks = local_blocks + jnp.einsum(
        "rb,rnd->bnd",
        block_pick.astype(jnp.float32),
        returned,
        precision=lax.Precision.HIGHEST,
        preferred_element_type=jnp.float32,
    )
    grad_nodes = local_blocks.reshape(node_count, features)
    shares = lax.psum_scatter(partial_grads, "dom", scatter_dimension=1, tiled=True)
    weight_grads = lax.psum(shares.astype(jnp.bfloat16), "traj").astype(jnp.float32)
    return (
        agg.astype(jnp.bfloat16)[None],
        grad_edges.astype(jnp.bfloat16)[None],
        grad_nodes.astype(jnp.bfloat16)[None],
        weight_grads,
    )


def solution(mesh):
    in_specs = (
        P("traj", "dom", None),
        P("traj", "dom", None),
        P("traj", "dom", None),
        P("traj", "dom", None),
        P(),
        P(),
        P(),
        P(),
        P("dom"),
        P("dom"),
        P("dom"),
        P("dom"),
    )
    out_specs = (
        P("traj", "dom", None),
        P("traj", "dom", None),
        P("traj", "dom", None),
        P(None, "dom", None),
    )
    return jax.shard_map(
        per_device, mesh=mesh, in_specs=in_specs, out_specs=out_specs, check_vma=False
    )
```

profile of v0, /device:TPU:64, one launch (start us, length us, event | category | flops | bytes accessed | tf_op | source)
XLA Modules:
  0.0 410.1 jit_solution(11833137365645740440)
XLA Ops:
  0.6 0.0 copy-start
  0.6 1.6 convolution_convert_fusion
  2.2 0.0 copy-start.11
  2.2 0.0 copy-start.12
  2.2 0.0 copy-start.8
  2.2 0.8 fusion.38
  3.0 0.0 copy-start.3
  3.0 0.0 copy-start.4
  3.0 0.7 copy.82
  3.7 1.9 collective-permute-start
  5.6 3.5 collective-permute-start.1
  9.2 4.5 %collective-permute-start.2 = (bf16[128,512]{1,0:T(8,128)(2,1)S(1)}, bf16[128,512]{1,0:T(8,128)(2,1)}, u32[]{:S(2)}, u32[]{:S(2)}) collective-permute-start(bf16[128,512]{1,0:T(8,128)(2,1)S(1)} %bitcast.98), channel_id=1, source_target_pairs={{0,4},{1,5},{2,6},{3,7},{4,0},{5,1},{6,2},{7,3},{8,12},{9,13},{10,... | collective-permute-start | bytes 393224 | tf_op jit(solution)/shard_map/ppermute | solution.py:10
  13.7 5.0 %collective-permute-start.3 = (bf16[128,512]{1,0:T(8,128)(2,1)S(1)}, bf16[128,512]{1,0:T(8,128)(2,1)}, u32[]{:S(2)}, u32[]{:S(2)}) collective-permute-start(bf16[128,512]{1,0:T(8,128)(2,1)S(1)} %bitcast.99), channel_id=1, source_target_pairs={{0,8},{1,9},{2,10},{3,11},{4,12},{5,13},{6,14},{7,15},{8,0},{9,1},... | collective-permute-start | bytes 393224 | tf_op jit(solution)/shard_map/ppermute | solution.py:10
  18.8 0.6 fusion.39
  19.4 2.5 compare_select_fusion.1
  21.9 0.3 convolution_convert_fusion.1
  22.3 0.4 fusion.12
  22.7 0.0 copy-start.15
  22.7 0.7 bitcast_dynamic-update-slice_fusion
  23.5 1.3 copy.50
  24.7 1.3 dynamic-slice.6
  26.7 1.6 constant_dynamic-update-slice_fusion.3
  28.2 1.6 constant_dynamic-update-slice_fusion.2
  29.8 1.6 constant_dynamic-update-slice_fusion.1
  31.3 1.6 constant_dynamic-update-slice_fusion
  32.9 1.7 fusion.3
  34.7 0.0 copy-start.6
  34.7 0.4 convolution_add_fusion.2
  35.1 0.6 copy-done.6
  35.7 0.4 convolution_add_fusion.1
  36.2 0.6 copy-done.14
  36.8 0.6 fusion.40
  37.4 0.2 multiply_reduce_fusion.1
  37.5 0.2 copy-done.10
  37.7 0.5 fusion.36
  38.3 0.3 multiply_convert_fusion
  38.6 0.7 fusion.4
  39.2 1.3 fusion.5
  40.5 0.4 fusion.17
  40.9 1.9 fusion
  42.8 1.5 convolution_bitcast_fusion
  44.3 1.5 convolution_bitcast_fusion.1
  45.8 0.5 convolution_bitcast_fusion.2
  46.3 0.5 copy-done.5
  46.8 1.4 convolution_bitcast_fusion.3
  48.3 2.0 copy.58
  50.3 4.2 %fusion.41 = (bf16[768,512]{1,0:T(8,128)(2,1)S(1)}, f32[768,512]{1,0:T(8,128)}) fusion(f32[768,512]{1,0:T(8,128)} %fusion, bf16[512,512]{1,0:T(8,128)(2,1)S(1)} %copy-done), kind=kOutput, calls=%fused_computation.85 | convolution fusion | flops 2416312320 | bytes 4456448 | tf_op jit(solution)/shard_map/dot_general | solution.py:26
  54.5 0.7 fusion.37
  55.2 4.7 %collective-permute-start.7 = (bf16[128,512]{1,0:T(8,128)(2,1)}, bf16[128,512]{1,0:T(8,128)(2,1)S(1)}, u32[]{:S(2)}, u32[]{:S(2)}) collective-permute-start(bf16[128,512]{1,0:T(8,128)(2,1)} %get-tuple-element.35), channel_id=1, source_target_pairs={{0,8},{1,9},{2,10},{3,11},{4,12},{5,13},{6,14},{7,15},{8,0},{9,1},... | collective-permute-start | bytes 393224 | tf_op jit(solution)/shard_map/ppermute | solution.py:10
  60.0 2.2 collective-permute-start.6
  62.2 2.4 collective-permute-start.5
  64.6 1.9 collective-permute-start.4
  66.5 2.4 pad_maximum_fusion
  69.0 5.5 %copy.57 = f32[4,512,512]{2,0,1:T(4,128)} copy(f32[4,512,512]{1,2,0:T(8,128)} %pad_maximum_fusion) | data formatting | bytes 8388608 | tf_op jit(solution)/shard_map/stack | solution.py:107
  74.4 296.8 %all-reduce.2 = bf16[4,512,512]{2,0,1:T(4,128)(2,1)} all-reduce(f32[4,512,512]{2,0,1:T(4,128)} %copy.57), channel_id=2, replica_groups=mesh['traj'=8,'dom'=64] {'dom'}, use_global_device_ids=true, to_apply=%region_4.5.clone | all-reduce | flops 1048576 | bytes 6291456
  371.2 0.8 dynamic-slice_convert_fusion
  372.0 32.1 %psum.7 = bf16[4,8,512]{2,0,1:T(4,128)(2,1)S(1)} all-reduce(bf16[4,8,512]{2,0,1:T(4,128)(2,1)S(1)} %dynamic-slice_convert_fusion), channel_id=1, replica_groups=mesh['traj'=8,'dom'=64] {'traj'}, use_global_device_ids=true, to_apply=%region_5.6 | all-reduce | flops 16384 | bytes 65536 | tf_op jit(solution)/shard_map/psum | solution.py:137
  404.1 0.6 copy.59
  404.8 1.6 convolution_add_fusion.4
  406.4 0.0 copy-start.13
  406.4 1.2 fusion.6
  407.6 1.1 pad_maximum_fusion.1
  408.8 0.5 fusion.19
  409.3 0.8 fusion.14
  (36 shorter events, 0.2 us)
Async XLA Ops:
  0.6 34.0 %copy-start = (bf16[512,512]{1,0:T(8,128)(2,1)S(1)}, bf16[512,512]{1,0:T(8,128)(2,1)}, u32[]{:S(2)}) copy-start(bf16[512,512]{1,0:T(8,128)(2,1)} %param.19) | copy-start | bytes 1572868
  2.2 16.6 %copy-start.11 = (s32[4]{0:T(128)S(1)}, s32[4]{0:T(128)}, u32[]{:S(2)}) copy-start(s32[4]{0:T(128)} %param.23) | copy-start | bytes 52
  2.2 19.7 %copy-start.12 = (s32[512]{0:T(512)S(1)}, s32[512]{0:T(512)}, u32[]{:S(2)}) copy-start(s32[512]{0:T(512)} %param.24) | copy-start | bytes 6148
  2.2 19.7 %copy-start.8 = (bf16[1,256,512]{2,1,0:T(8,128)(2,1)S(1)}, bf16[1,256,512]{2,1,0:T(8,128)(2,1)}, u32[]{:S(2)}) copy-start(bf16[1,256,512]{2,1,0:T(8,128)(2,1)} %param.14) | copy-start | bytes 786436
  3.0 19.3 %copy-start.3 = (bf16[512,512]{1,0:T(8,128)(2,1)S(1)}, bf16[512,512]{1,0:T(8,128)(2,1)}, u32[]{:S(2)}) copy-start(bf16[512,512]{1,0:T(8,128)(2,1)} %param.18) | copy-start | bytes 1572868
  3.0 19.3 %copy-start.4 = (bf16[1,512,512]{2,1,0:T(8,128)(2,1)S(1)}, bf16[1,512,512]{2,1,0:T(8,128)(2,1)}, u32[]{:S(2)}) copy-start(bf16[1,512,512]{2,1,0:T(8,128)(2,1)} %param.15) | copy-start | bytes 1572868
  3.7 22.9 %collective-permute-start = (bf16[128,512]{1,0:T(8,128)(2,1)}, bf16[128,512]{1,0:T(8,128)(2,1)}, u32[]{:S(2)}, u32[]{:S(2)}) collective-permute-start(bf16[128,512]{1,0:T(8,128)(2,1)} %bitcast.94), channel_id=1, source_target_pairs={{0,1},{1,0},{2,3},{3,2},{4,5},{5,4},{6,7},{7,6},{8,9},{9,8},{10,11... | collective-permute-start | bytes 393224 | tf_op jit(solution)/shard_map/ppermute | solution.py:10
  5.6 22.6 %collective-permute-start.1 = (bf16[128,512]{1,0:T(8,128)(2,1)S(1)}, bf16[128,512]{1,0:T(8,128)(2,1)}, u32[]{:S(2)}, u32[]{:S(2)}) collective-permute-start(bf16[128,512]{1,0:T(8,128)(2,1)S(1)} %bitcast.100), channel_id=1, source_target_pairs={{0,2},{1,3},{2,0},{3,1},{4,6},{5,7},{6,4},{7,5},{8,10},{9,11},{10,... | collective-permute-start | bytes 393224 | tf_op jit(solution)/shard_map/ppermute | solution.py:10
  9.2 20.6 %collective-permute-start.2 = (bf16[128,512]{1,0:T(8,128)(2,1)S(1)}, bf16[128,512]{1,0:T(8,128)(2,1)}, u32[]{:S(2)}, u32[]{:S(2)}) collective-permute-start(bf16[128,512]{1,0:T(8,128)(2,1)S(1)} %bitcast.98), channel_id=1, source_target_pairs={{0,4},{1,5},{2,6},{3,7},{4,0},{5,1},{6,2},{7,3},{8,12},{9,13},{10,... | collective-permute-start | bytes 393224 | tf_op jit(solution)/shard_map/ppermute | solution.py:10
  13.7 17.6 %collective-permute-start.3 = (bf16[128,512]{1,0:T(8,128)(2,1)S(1)}, bf16[128,512]{1,0:T(8,128)(2,1)}, u32[]{:S(2)}, u32[]{:S(2)}) collective-permute-start(bf16[128,512]{1,0:T(8,128)(2,1)S(1)} %bitcast.99), channel_id=1, source_target_pairs={{0,8},{1,9},{2,10},{3,11},{4,12},{5,13},{6,14},{7,15},{8,0},{9,1},... | collective-permute-start | bytes 393224 | tf_op jit(solution)/shard_map/ppermute | solution.py:10
  22.7 10.2 %copy-start.15 = (s32[512]{0:T(512)S(1)}, s32[512]{0:T(512)}, u32[]{:S(2)}) copy-start(s32[512]{0:T(512)} %param.22) | copy-start | bytes 6148
  34.7 1.0 copy-start.6
  35.7 1.0 copy-start.14
  36.8 0.9 copy-start.10
  45.8 1.0 copy-start.5
  50.3 16.2 %copy-start.2 = (f32[1,512,512]{1,2,0:T(8,128)S(1)}, f32[1,512,512]{1,2,0:T(8,128)}, u32[]{:S(2)}) copy-start(f32[1,512,512]{1,2,0:T(8,128)} %convolution_bitcast_fusion.3) | copy-start | bytes 3145732
  50.3 16.2 %copy-start.9 = (f32[1,512,512]{1,2,0:T(8,128)S(1)}, f32[1,512,512]{1,2,0:T(8,128)}, u32[]{:S(2)}) copy-start(f32[1,512,512]{1,2,0:T(8,128)} %convolution_bitcast_fusion) | copy-start | bytes 3145732
  54.5 12.0 %copy-start.1 = (f32[1,512,512]{1,2,0:T(8,128)S(1)}, f32[1,512,512]{1,2,0:T(8,128)}, u32[]{:S(2)}) copy-start(f32[1,512,512]{1,2,0:T(8,128)} %convolution_bitcast_fusion.1) | copy-start | bytes 3145732
  55.2 352.4 %collective-permute-start.7 = (bf16[128,512]{1,0:T(8,128)(2,1)}, bf16[128,512]{1,0:T(8,128)(2,1)S(1)}, u32[]{:S(2)}, u32[]{:S(2)}) collective-permute-start(bf16[128,512]{1,0:T(8,128)(2,1)} %get-tuple-element.35), channel_id=1, source_target_pairs={{0,8},{1,9},{2,10},{3,11},{4,12},{5,13},{6,14},{7,15},{8,0},{9,1},... | collective-permute-start | bytes 393224 | tf_op jit(solution)/shard_map/ppermute | solution.py:10
  60.0 347.7 %collective-permute-start.6 = (bf16[128,512]{1,0:T(8,128)(2,1)}, bf16[128,512]{1,0:T(8,128)(2,1)}, u32[]{:S(2)}, u32[]{:S(2)}) collective-permute-start(bf16[128,512]{1,0:T(8,128)(2,1)} %get-tuple-element.36), channel_id=1, source_target_pairs={{0,4},{1,5},{2,6},{3,7},{4,0},{5,1},{6,2},{7,3},{8,12},{9,13},{10,... | collective-permute-start | bytes 393224 | tf_op jit(solution)/shard_map/ppermute | solution.py:10
  62.2 345.4 %collective-permute-start.5 = (bf16[128,512]{1,0:T(8,128)(2,1)S(1)}, bf16[128,512]{1,0:T(8,128)(2,1)}, u32[]{:S(2)}, u32[]{:S(2)}) collective-permute-start(bf16[128,512]{1,0:T(8,128)(2,1)S(1)} %get-tuple-element.37), channel_id=1, source_target_pairs={{0,2},{1,3},{2,0},{3,1},{4,6},{5,7},{6,4},{7,5},{8,10},{9,11},{10,... | collective-permute-start | bytes 393224 | tf_op jit(solution)/shard_map/ppermute | solution.py:10
  64.6 343.1 %collective-permute-start.4 = (bf16[128,512]{1,0:T(8,128)(2,1)S(1)}, bf16[128,512]{1,0:T(8,128)(2,1)}, u32[]{:S(2)}, u32[]{:S(2)}) collective-permute-start(bf16[128,512]{1,0:T(8,128)(2,1)S(1)} %get-tuple-element.34), channel_id=1, source_target_pairs={{0,1},{1,0},{2,3},{3,2},{4,5},{5,4},{6,7},{7,6},{8,9},{9,8},{10,11... | collective-permute-start | bytes 393224 | tf_op jit(solution)/shard_map/ppermute | solution.py:10
  74.4 330.4 %copy-start.7 = (bf16[512,512]{1,0:T(8,128)(2,1)S(1)}, bf16[512,512]{1,0:T(8,128)(2,1)}, u32[]{:S(2)}) copy-start(bf16[512,512]{1,0:T(8,128)(2,1)} %param.20) | copy-start | bytes 1572868
  406.4 2.3 copy-start.13
where the time goes:
time: 411 us; the launch traced here: 410 us
  blocking collectives  329 us (80%)
  starting transfers between devices  26.2 us (6%)
  local copies, waits for them, and re-layouts  23.2 us (6%)
  matrix products  22.7 us (6%)
  other arithmetic  7.34 us (2%)
    unnamed x1, blocking collectives  297 us
    psum x1, blocking collectives, per_device(): lax.psum(shares.astype(jnp.bfloat16), 'traj').astype(jnp.float32)  32.1 us
    ppermute x8, starting transfers between devices, partner(): lax.ppermute(shard, axis, [(i, i ^ 1 << stride) for i in range(lax.axis_s...  26.2 us
    unnamed x44, local copies, waits for them, and re-layouts  13.3 us
    dot_general x7, matrix products, dot_rows(): lax.dot_general(former, latter, (((0,), (0,)), ((), ())), preferred_eleme...  8.39 us
  transfers between devices with their start and end apart: 8, of which 0 were waited for; matrix products, arithmetic and copies ran while one was open for 6% of the time, Pallas kernels for 0%

commit v1 on v0

v1 whole, which is shorter than its diff:
```python
import jax
import jax.numpy as jnp
from jax import lax
from jax.experimental import pallas as pl
from jax.experimental.pallas import tpu as pltpu
from jax.sharding import PartitionSpec as P

ROUNDS = 4
F32 = jnp.float32
BF16 = jnp.bfloat16
MESH = pl.DeviceIdType.MESH
CHUNKS = (("xz", 0, 80), ("zx", 80, 48))


def mm(a, b):
    return jnp.dot(a, b, preferred_element_type=F32)


def mm_tn(a, b):
    return lax.dot_general(a, b, (((0,), (0,)), ((), ())), preferred_element_type=F32)


def mm_nt(a, b):
    return lax.dot_general(a, b, (((1,), (1,)), ((), ())), preferred_element_type=F32)


def kernel(
    node_h, edge_h, ge_h, ga_h, we_h, ws_h, wr_h, wo_h, src_h, rblk_h, rnode_h, sblk_h,
    agg_o, gedge_o, gnode_o, wg_o,
    table, edge, ge, ga, we, ws, wr, wo, src, rnode, rblk, sblk,
    lent, oh, oht, rh, rht, pre, gmsg, srows, hid, msg, gproj, gpre, slot_out, slot_in,
    part, core_in, quart, x_in0, z_in0, mid0, x_in1, z_in1, mid1, sums, y_in, fin, gath,
    agg_v, gedge_v, gnode_v,
    ld, ex_s, ex_r, rt_s, rt_r, co_s, co_r, xs_s, xs_r, zs_s, zs_r, ys_s, ys_r, ag_s, ag_r, st,
):
    t = lax.axis_index("traj")
    d = lax.axis_index("dom")
    x, y, c = d // 16, (d // 2) % 8, d % 2

    def dom(xx, yy, cc):
        return xx * 16 + yy * 2 + cc

    partners = [(t, d + 1 - 2 * c)]
    for r in range(1, ROUNDS):
        h = 1 << (r - 1)
        partners.append((t, dom(x, y + h - 2 * h * ((y // h) % 2), c)))
    x_peer = [(t, dom((x + k) % 4, y, c)) for k in range(1, 4)]
    y_peer = [(t, dom(x, (y + k) % 8, c)) for k in range(1, 8)]
    z_peer = [((t + k) % 8, d) for k in range(1, 8)]
    g_peer = z_peer + [((t + k) % 8, dom(x, y, 1 - c)) for k in range(8)]

    loads = {}

    def load(i, s, dst):
        loads[i] = pltpu.make_async_copy(s, dst, ld.at[i])
        loads[i].start()

    load(0, node_h.at[0], table.at[0:256])
    load(1, sblk_h, sblk)
    load(2, src_h, src)
    load(3, rblk_h, rblk)
    load(4, rnode_h, rnode)
    load(5, edge_h.at[0], edge)
    load(6, we_h, we)
    load(7, wr_h, wr)
    load(8, ga_h.at[0], ga)
    load(9, ge_h.at[0], ge)
    load(10, ws_h, ws)
    load(11, wo_h, wo)

    bar = pltpu.get_barrier_semaphore()
    greet = [partners[0]] + y_peer + x_peer + g_peer[:7] + g_peer[8:]
    for dev in greet:
        pl.semaphore_signal(bar, inc=1, device_id=dev, device_id_type=MESH)

    def remote(s, dst, ss, rs, dev):
        cp = pltpu.make_async_remote_copy(
            src_ref=s, dst_ref=dst, send_sem=ss, recv_sem=rs, device_id=dev, device_id_type=MESH
        )
        cp.start()
        return cp

    loads[0].wait()
    loads[1].wait()
    for r in range(ROUNDS):
        pick = jnp.broadcast_to(sblk[:, r : r + 1], (128, 512)) == 0
        lent[r] = jnp.where(pick, table[0:128, :].astype(F32), table[128:256, :].astype(F32)).astype(BF16)
    pl.semaphore_wait(bar, len(greet))
    ex = {}
    for r in (3, 2, 1, 0):
        ex[r] = remote(
            lent.at[r], table.at[256 + 128 * r : 384 + 128 * r], ex_s.at[r], ex_r.at[r], partners[r]
        )

    for i in (2, 3, 4):
        loads[i].wait()
    slots = lax.broadcasted_iota(jnp.int32, (768, 512), 0)
    oht[...] = (slots == src[...]).astype(F32).astype(BF16)
    own = lax.broadcasted_iota(jnp.int32, (256, 128), 0)
    for j in range(4):
        hit = own == rnode[:, 128 * j : 128 * (j + 1)] + rblk[:, j : j + 1] * 128
        rht[:, 128 * j : 128 * (j + 1)] = hit.astype(F32).astype(BF16)
    oh[...] = oht[...].T
    rh[...] = rht[...].T
    for i in (5, 6, 7, 8, 9):
        loads[i].wait()
    for e in (0, 256):
        rows = slice(e, e + 256)
        rrows = mm(rh[rows, :], table[0:256, :]).astype(BF16)
        pre[rows, :] = mm(edge[rows, :], we[...]) + mm(rrows, wr[...])
        gmsg[rows, :] = ge[rows, :].astype(F32) + mm(rh[rows, :], ga[...])
    for i in (10, 11):
        loads[i].wait()

    for r in range(ROUNDS):
        ex[r].wait_recv()

    for e in (0, 256):
        rows = slice(e, e + 256)
        sr = mm(oh[rows, :], table[...]).astype(BF16)
        srows[rows, :] = sr
        p = pre[rows, :] + mm(sr, ws[...])
        sig = 1.0 / (1.0 + jnp.exp(-p))
        hv = (p * sig).astype(BF16)
        hid[rows, :] = hv
        dsilu = sig * (1.0 + p * (1.0 - sig))
        proj = mm(hv, wo[...])
        cen = proj - jnp.mean(proj, axis=1, keepdims=True)
        inv = lax.rsqrt(jnp.mean(cen * cen, axis=1, keepdims=True) + 1e-05)
        nrm = cen * inv
        msg[rows, :] = nrm.astype(BF16)
        g = gmsg[rows, :]
        gp = inv * (
            g - jnp.mean(g, axis=1, keepdims=True) - nrm * jnp.mean(g * nrm, axis=1, keepdims=True)
        )
        gp = gp.astype(BF16)
        gproj[rows, :] = gp
        gpre[rows, :] = (mm_nt(gp, wo[...]) * dsilu).astype(BF16)

    ret = {}
    for r in (3, 2, 1, 0):
        rows = slice(256 + 128 * r, 384 + 128 * r)
        slot_out[r] = mm(oht[rows, :], gpre[...]).astype(BF16)
        ret[r] = remote(slot_out.at[r], slot_in.at[r], rt_s.at[r], rt_r.at[r], partners[r])

    core = []
    for m in range(4):
        lhs = (edge, srows, None, hid)[m]
        rhs = (gpre, gpre, None, gproj)[m]
        if m == 2:
            rsum = mm(rht[...], gpre[...]).astype(BF16)
            gw = mm_tn(table[0:256, :], rsum)
        else:
            gw = mm_tn(lhs[...], rhs[...])
        gw = gw.astype(BF16)
        for xx in range(4):
            for b in range(4):
                part[b // 2, xx, 2 * m + b % 2] = gw[128 * xx : 128 * (xx + 1), 128 * b : 128 * (b + 1)]
        core.append(
            remote(
                part.at[1 - c, :, 2 * m : 2 * m + 2],
                core_in.at[:, 2 * m : 2 * m + 2],
                co_s.at[m],
                co_r.at[m],
                partners[0],
            )
        )
    for m in range(4):
        core[m].wait_recv()
        z2 = slice(2 * m, 2 * m + 2)
        quart[:, z2] = (part[c, :, z2].astype(F32) + core_in[:, z2].astype(F32)).astype(BF16)

    bufs = ((x_in0, z_in0, mid0), (x_in1, z_in1, mid1))
    first, second = [], []
    for i, (order, lo, n) in enumerate(CHUNKS):
        xi, zi, _ = bufs[i]
        rs = slice(lo, lo + n)
        sent = []
        if order == "xz":
            for k in (2, 1, 3):
                sent.append(
                    remote(
                        quart.at[(x + k) % 4, :, rs], xi.at[k - 1],
                        xs_s.at[i, k - 1], xs_r.at[i, k - 1], x_peer[k - 1],
                    )
                )
        else:
            for k in (4, 3, 5, 2, 6, 1, 7):
                sent.append(
                    remote(
                        quart.at[:, (t + k) % 8, rs], zi.at[k - 1],
                        zs_s.at[i, k - 1], zs_r.at[i, k - 1], z_peer[k - 1],
                    )
                )
        first.append(sent)

    agg_v[...] = mm(rht[...], msg[...]).astype(BF16)
    out0 = pltpu.make_async_copy(agg_v, agg_o.at[0], st.at[0])
    out0.start()
    for e in (0, 256):
        rows = slice(e, e + 256)
        gedge_v[rows, :] = (ge[rows, :].astype(F32) + mm_nt(gpre[rows, :], we[...])).astype(BF16)
    out1 = pltpu.make_async_copy(gedge_v, gedge_o.at[0], st.at[1])
    out1.start()
    own_sum = [mm(oht[128 * b : 128 * (b + 1), :], gpre[...]) for b in range(2)]
    gn_recv = mm_nt(rsum, wr[...])

    for i, (order, lo, n) in enumerate(CHUNKS):
        xi, zi, mid = bufs[i]
        rs = slice(lo, lo + n)
        for cp in first[i]:
            cp.wait_recv()
        sent = []
        if order == "xz":
            acc = quart[x, :, rs].astype(F32)
            for k in range(3):
                acc = acc + xi[k].astype(F32)
            mid[...] = acc.astype(BF16)
            for k in (4, 3, 5, 2, 6, 1, 7):
                sent.append(
                    remote(
                        mid.at[(t + k) % 8], zi.at[k - 1],
                        zs_s.at[i, k - 1], zs_r.at[i, k - 1], z_peer[k - 1],
                    )
                )
        else:
            acc = quart[:, t, rs].astype(F32)
            for k in range(7):
                acc = acc + zi[k].astype(F32)
            mid[...] = acc.astype(BF16)
            for k in (2, 1, 3):
                sent.append(
                    remote(
                        mid.at[(x + k) % 4], xi.at[k - 1],
                        xs_s.at[i, k - 1], xs_r.at[i, k - 1], x_peer[k - 1],
                    )
                )
        second.append(sent)

    for r in range(ROUNDS):
        ret[r].wait_recv()
        v = slot_in[r].astype(F32)
        for b in range(2):
            own_sum[b] = own_sum[b] + v * (sblk[:, r : r + 1] == b).astype(F32)
    for b in range(2):
        rows = slice(128 * b, 128 * (b + 1))
        gn = gn_recv[rows, :] + mm_nt(own_sum[b].astype(BF16), ws[...])
        gnode_v[rows, :] = gn.astype(BF16)
    out2 = pltpu.make_async_copy(gnode_v, gnode_o.at[0], st.at[2])
    out2.start()

    for i, (order, lo, n) in enumerate(CHUNKS):
        xi, zi, mid = bufs[i]
        for cp in second[i]:
            cp.wait_recv()
        if order == "xz":
            acc = mid[t].astype(F32)
            for k in range(7):
                acc = acc + zi[k].astype(F32)
        else:
            acc = mid[x].astype(F32)
            for k in range(3):
                acc = acc + xi[k].astype(F32)
        for j in range(n // 16):
            sums[lo // 16 + j] = acc[16 * j : 16 * (j + 1), :].astype(BF16)

    ysent = []
    for k in (4, 3, 5, 2, 6, 1, 7):
        ysent.append(
            remote(sums.at[(y + k) % 8], y_in.at[k - 1], ys_s.at[k - 1], ys_r.at[k - 1], y_peer[k - 1])
        )
    for cp in ysent:
        cp.wait_recv()
    acc = sums[y].astype(F32)
    for k in range(7):
        acc = acc + y_in[k].astype(F32)
    fin[0] = acc[0:8, :]
    fin[1] = acc[8:16, :]
    slot = (t // 2, 2 * c + t % 2)
    gsent = []
    for i, dev in enumerate(g_peer):
        half = c if i < 7 else 1 - c
        gsent.append(remote(fin.at[half], gath.at[slot[0], slot[1]], ag_s.at[i], ag_r.at[i], dev))
    mine = pltpu.make_async_copy(fin.at[c], gath.at[slot[0], slot[1]], st.at[3])
    mine.start()
    mine.wait()
    for cp in gsent:
        cp.wait_recv()
    for b in range(4):
        wg_o[:, :, 128 * b : 128 * (b + 1)] = gath[:, b]

    for r in range(ROUNDS):
        ex[r].wait_send()
        ret[r].wait_send()
    for cp in core + first[0] + first[1] + second[0] + second[1] + ysent + gsent:
        cp.wait_send()
    out0.wait()
    out1.wait()
    out2.wait()


def per_device(
    node_lat, edge_lat, grad_edge, grad_agg, weight_edge, weight_send, weight_recv, weight_out,
    edge_src, edge_recv_block, edge_recv_node, send_blocks,
):
    vm, dma = pltpu.VMEM, pltpu.SemaphoreType.DMA
    big = (512, 512)
    scratch = [
        vm((768, 512), BF16), vm(big, BF16), vm(big, BF16), vm((256, 512), BF16),
        vm(big, BF16), vm(big, BF16), vm(big, BF16), vm(big, BF16),
        vm((1, 512), jnp.int32), vm((1, 512), jnp.int32),
        vm((1, 4), jnp.int32), vm((1, 4), jnp.int32),
        vm((4, 128, 512), BF16), vm((512, 768), BF16), vm((768, 512), BF16),
        vm((512, 256), BF16), vm((256, 512), BF16),
        vm(big, F32), vm(big, F32),
        vm(big, BF16), vm(big, BF16), vm(big, BF16), vm(big, BF16), vm(big, BF16),
        vm((4, 128, 512), BF16), vm((4, 128, 512), BF16),
        vm((2, 4, 8, 128, 128), BF16), vm((4, 8, 128, 128), BF16), vm((4, 8, 128, 128), BF16),
    ]
    for order, _, n in CHUNKS:
        if order == "xz":
            scratch += [vm((3, 8, n, 128), BF16), vm((7, n, 128), BF16), vm((8, n, 128), BF16)]
        else:
            scratch += [vm((3, n, 128), BF16), vm((7, 4, n, 128), BF16), vm((4, n, 128), BF16)]
    scratch += [
        vm((8, 16, 128), BF16), vm((7, 16, 128), BF16), vm((2, 8, 128), F32), vm((4, 4, 8, 128), F32),
        vm((256, 512), BF16), vm(big, BF16), vm((256, 512), BF16),
        dma((12,)), dma((4,)), dma((4,)), dma((4,)), dma((4,)), dma((4,)), dma((4,)),
        dma((2, 3)), dma((2, 3)), dma((2, 7)), dma((2, 7)), dma((7,)), dma((7,)),
        dma((15,)), dma((15,)), dma((4,)),
    ]
    hbm = pl.BlockSpec(memory_space=pl.ANY)
    return pl.pallas_call(
        kernel,
        out_shape=(
            jax.ShapeDtypeStruct((1, 256, 512), BF16),
            jax.ShapeDtypeStruct((1, 512, 512), BF16),
            jax.ShapeDtypeStruct((1, 256, 512), BF16),
            jax.ShapeDtypeStruct((4, 8, 512), F32),
        ),
        in_specs=[hbm] * 12,
        out_specs=(hbm, hbm, hbm, pl.BlockSpec(memory_space=pltpu.VMEM)),
        scratch_shapes=scratch,
        compiler_params=pltpu.CompilerParams(
            collective_id=0, has_side_effects=True, vmem_limit_bytes=56 << 20
        ),
        name="edge_update_backward",
    )(
        node_lat, edge_lat, grad_edge, grad_agg, weight_edge, weight_send, weight_recv, weight_out,
        edge_src.reshape(1, 512), edge_recv_block.reshape(1, 4),
        edge_recv_node.reshape(1, 512), send_blocks.reshape(1, 4),
    )


def solution(mesh):
    lat = P("traj", "dom", None)
    return jax.shard_map(
        per_device,
        mesh=mesh,
        in_specs=(lat,) * 4 + (P(),) * 4 + (P("dom"),) * 4,
        out_specs=(lat, lat, lat, P(None, "dom", None)),
        check_vma=False,
    )
```

time: 411 us -> 67.9 us (0.17)
  the two profiles are of different devices: /device:TPU:64 before, /device:TPU:1 now
where the time goes in v1:
time: 67.9 us; the launch traced here: 67.7 us
  Pallas kernels  62.7 us (92%)
  local copies, waits for them, and re-layouts  4.31 us (6%)
    pallas_call x1, Pallas kernels, per_device(): pl.pallas_call(kernel, out_shape=(jax.ShapeDtypeStruct((1, 256, 512), BF1...  62.7 us
    unnamed x10, local copies, waits for them, and re-layouts  4.31 us

profile of v1, /device:TPU:1, one launch (start us, length us, event | category | flops | bytes accessed | tf_op | source)
XLA Modules:
  0.0 67.7 jit_solution(1504529333722280369)
XLA Ops:
  0.6 62.7 %edge_update_backward.1 = (bf16[1,256,512]{2,1,0:T(8,128)(2,1)}, bf16[1,512,512]{2,1,0:T(8,128)(2,1)}, bf16[1,256,512]{2,1,0:T(8,128)(2,1)}, f32[4,8,512]{2,1,0:T(8,128)}) custom-call(bf16[1,256,512]{2,1,0:T(8,128)(2,1)} %node_h.1, bf16[1,512,512]{2,1,0:T(8,128)(2,1)} %edge_h.1, bf16[1,512,512]{2,1,0:T(8,128)(2,1)} %ge_h.1, bf16[1,256,512]{2,1,0:T(8,128)(2,1)} %ga_h.1, ...), custom_call_target="tpu_custom_call" | custom-call | tf_op jit(solution)/shard_map/edge_update_backward/pallas_call | solution.py:333
  63.4 0.0 copy-start
  63.4 1.7 %copy.20 = bf16[1,256,512]{2,1,0:T(8,128)(2,1)} copy(bf16[1,256,512]{2,1,0:T(8,128)(2,1)} %get-tuple-element.8) | data formatting | bytes 524288
  65.1 0.0 copy-done
  65.1 0.0 copy-start.1
  65.1 0.8 %copy.21 = bf16[1,512,512]{2,1,0:T(8,128)(2,1)} copy(bf16[1,512,512]{2,1,0:T(8,128)(2,1)S(1)} %copy-done) | data formatting | bytes 1048576
  65.9 0.3 copy-done.1
  66.2 0.0 copy-start.2
  66.2 0.7 %copy.22 = bf16[1,256,512]{2,1,0:T(8,128)(2,1)} copy(bf16[1,256,512]{2,1,0:T(8,128)(2,1)S(1)} %copy-done.1) | data formatting | bytes 524288
  66.9 0.2 copy-done.2
  67.1 0.6 copy.23
Async XLA Ops:
  63.4 1.7 %copy-start = (bf16[1,512,512]{2,1,0:T(8,128)(2,1)S(1)}, bf16[1,512,512]{2,1,0:T(8,128)(2,1)}, u32[]{:S(2)}) copy-start(bf16[1,512,512]{2,1,0:T(8,128)(2,1)} %get-tuple-element.9) | copy-start | bytes 1572868
  65.1 1.1 %copy-start.1 = (bf16[1,256,512]{2,1,0:T(8,128)(2,1)S(1)}, bf16[1,256,512]{2,1,0:T(8,128)(2,1)}, u32[]{:S(2)}) copy-start(bf16[1,256,512]{2,1,0:T(8,128)(2,1)} %get-tuple-element.10) | copy-start | bytes 786436
  66.2 0.9 %copy-start.2 = (f32[4,8,512]{2,1,0:T(8,128)S(1)}, f32[4,8,512]{2,1,0:T(8,128)}, u32[]{:S(2)}) copy-start(f32[4,8,512]{2,1,0:T(8,128)} %get-tuple-element.11) | copy-start | bytes 196612

commit v2 on v1

--- a/solution.py
+++ b/solution.py
@@ -9,7 +9,7 @@
 F32 = jnp.float32
 BF16 = jnp.bfloat16
 MESH = pl.DeviceIdType.MESH
-CHUNKS = (("xz", 0, 80), ("zx", 80, 48))
+CHUNKS = (("xz", 0, 32), ("zx", 48, 16), ("xz", 32, 16))
 
 
 def mm(a, b):
@@ -29,7 +29,7 @@
     agg_o, gedge_o, gnode_o, wg_o,
     table, edge, ge, ga, we, ws, wr, wo, src, rnode, rblk, sblk,
     lent, oh, oht, rh, rht, pre, gmsg, srows, hid, msg, gproj, gpre, slot_out, slot_in,
-    part, core_in, quart, x_in0, z_in0, mid0, x_in1, z_in1, mid1, sums, y_in, fin, gath,
+    rsum, part, core_in, quart, x_in0, z_in0, mid0, x_in1, z_in1, mid1, x_in2, z_in2, mid2, sums, y_in, fin, gath,
     agg_v, gedge_v, gnode_v,
     ld, ex_s, ex_r, rt_s, rt_r, co_s, co_r, xs_s, xs_r, zs_s, zs_r, ys_s, ys_r, ag_s, ag_r, st,
 ):
@@ -47,9 +47,8 @@
     x_peer = [(t, dom((x + k) % 4, y, c)) for k in range(1, 4)]
     y_peer = [(t, dom(x, (y + k) % 8, c)) for k in range(1, 8)]
     z_peer = [((t + k) % 8, d) for k in range(1, 8)]
-    g_peer = z_peer + [((t + k) % 8, dom(x, y, 1 - c)) for k in range(8)]
-
-    loads = {}
+
+    loads, started, taken = {}, [], set()
 
     def load(i, s, dst):
         loads[i] = pltpu.make_async_copy(s, dst, ld.at[i])
@@ -69,7 +68,7 @@
     load(11, wo_h, wo)
 
     bar = pltpu.get_barrier_semaphore()
-    greet = [partners[0]] + y_peer + x_peer + g_peer[:7] + g_peer[8:]
+    greet = [partners[0]] + y_peer + x_peer + z_peer
     for dev in greet:
         pl.semaphore_signal(bar, inc=1, device_id=dev, device_id_type=MESH)
 
@@ -78,7 +77,12 @@
             src_ref=s, dst_ref=dst, send_sem=ss, recv_sem=rs, device_id=dev, device_id_type=MESH
         )
         cp.start()
+        started.append(cp)
         return cp
+
+    def take(cp):
+        cp.wait_recv()
+        taken.add(id(cp))
 
     loads[0].wait()
     loads[1].wait()
@@ -113,7 +117,7 @@
         loads[i].wait()
 
     for r in range(ROUNDS):
-        ex[r].wait_recv()
+        take(ex[r])
 
     for e in (0, 256):
         rows = slice(e, e + 256)
@@ -137,25 +141,25 @@
         gproj[rows, :] = gp
         gpre[rows, :] = (mm_nt(gp, wo[...]) * dsilu).astype(BF16)
 
-    ret = {}
-    for r in (3, 2, 1, 0):
-        rows = slice(256 + 128 * r, 384 + 128 * r)
-        slot_out[r] = mm(oht[rows, :], gpre[...]).astype(BF16)
-        ret[r] = remote(slot_out.at[r], slot_in.at[r], rt_s.at[r], rt_r.at[r], partners[r])
-
-    core = []
-    for m in range(4):
-        lhs = (edge, srows, None, hid)[m]
-        rhs = (gpre, gpre, None, gproj)[m]
-        if m == 2:
-            rsum = mm(rht[...], gpre[...]).astype(BF16)
-            gw = mm_tn(table[0:256, :], rsum)
+    core, ret = [], {}
+    bufs = ((x_in0, z_in0, mid0), (x_in1, z_in1, mid1), (x_in2, z_in2, mid2))
+    first = [[] for _ in CHUNKS]
+
+    def grad(m):
+        if m == 0:
+            gw = mm_tn(edge[...], gpre[...])
+        elif m == 1:
+            gw = mm_tn(srows[...], gpre[...])
+        elif m == 2:
+            gw = mm_tn(table[0:256, :], rsum[...])
         else:
-            gw = mm_tn(lhs[...], rhs[...])
-        gw = gw.astype(BF16)
+            gw = mm_tn(hid[...], gproj[...])
+        gw = gw.reshape(4, 8, 2, 8, 512)
         for xx in range(4):
-            for b in range(4):
-                part[b // 2, xx, 2 * m + b % 2] = gw[128 * xx : 128 * (xx + 1), 128 * b : 128 * (b + 1)]
+            for cc in range(2):
+                v = gw[xx, :, cc].reshape(64, 512).astype(BF16)
+                part[cc, xx, 2 * m] = v[:, 0:256]
+                part[cc, xx, 2 * m + 1] = v[:, 256:512]
         core.append(
             remote(
                 part.at[1 - c, :, 2 * m : 2 * m + 2],
@@ -165,34 +169,51 @@
                 partners[0],
             )
         )
-    for m in range(4):
-        core[m].wait_recv()
+
+    def merge(m):
+        take(core[m])
         z2 = slice(2 * m, 2 * m + 2)
         quart[:, z2] = (part[c, :, z2].astype(F32) + core_in[:, z2].astype(F32)).astype(BF16)
 
-    bufs = ((x_in0, z_in0, mid0), (x_in1, z_in1, mid1))
-    first, second = [], []
-    for i, (order, lo, n) in enumerate(CHUNKS):
-        xi, zi, _ = bufs[i]
-        rs = slice(lo, lo + n)
-        sent = []
-        if order == "xz":
-            for k in (2, 1, 3):
-                sent.append(
-                    remote(
-                        quart.at[(x + k) % 4, :, rs], xi.at[k - 1],
-                        xs_s.at[i, k - 1], xs_r.at[i, k - 1], x_peer[k - 1],
-                    )
+    def send_x(i, g):
+        _, lo, n = CHUNKS[i]
+        zs = slice(4 * g, 4 * g + 4)
+        for k in (2, 1, 3):
+            first[i].append(
+                remote(
+                    quart.at[(x + k) % 4, zs, lo : lo + n], bufs[i][0].at[k - 1, zs],
+                    xs_s.at[i, g, k - 1], xs_r.at[i, g, k - 1], x_peer[k - 1],
                 )
-        else:
-            for k in (4, 3, 5, 2, 6, 1, 7):
-                sent.append(
-                    remote(
-                        quart.at[:, (t + k) % 8, rs], zi.at[k - 1],
-                        zs_s.at[i, k - 1], zs_r.at[i, k - 1], z_peer[k - 1],
-                    )
+            )
+
+    def send_z(i):
+        _, lo, n = CHUNKS[i]
+        for k in (4, 3, 5, 2, 6, 1, 7):
+            first[i].append(
+                remote(
+                    quart.at[:, (t + k) % 8, lo : lo + n], bufs[i][1].at[k - 1],
+                    zs_s.at[i, k - 1], zs_r.at[i, k - 1], z_peer[k - 1],
                 )
-        first.append(sent)
+            )
+
+    grad(0)
+    grad(1)
+    rsum[...] = mm(rht[...], gpre[...]).astype(BF16)
+    grad(2)
+    merge(0)
+    merge(1)
+    send_x(0, 0)
+    grad(3)
+    for r in (3, 2, 1, 0):
+        rows = slice(256 + 128 * r, 384 + 128 * r)
+        slot_out[r] = mm(oht[rows, :], gpre[...]).astype(BF16)
+        ret[r] = remote(slot_out.at[r], slot_in.at[r], rt_s.at[r], rt_r.at[r], partners[r])
+    merge(2)
+    merge(3)
+    send_z(1)
+    send_x(0, 1)
+    send_x(2, 0)
+    send_x(2, 1)
 
     agg_v[...] = mm(rht[...], msg[...]).astype(BF16)
     out0 = pltpu.make_async_copy(agg_v, agg_o.at[0], st.at[0])
@@ -203,13 +224,14 @@
     out1 = pltpu.make_async_copy(gedge_v, gedge_o.at[0], st.at[1])
     out1.start()
     own_sum = [mm(oht[128 * b : 128 * (b + 1), :], gpre[...]) for b in range(2)]
-    gn_recv = mm_nt(rsum, wr[...])
-
+    gn_recv = mm_nt(rsum[...], wr[...])
+
+    second = []
     for i, (order, lo, n) in enumerate(CHUNKS):
         xi, zi, mid = bufs[i]
         rs = slice(lo, lo + n)
         for cp in first[i]:
-            cp.wait_recv()
+            take(cp)
         sent = []
         if order == "xz":
             acc = quart[x, :, rs].astype(F32)
@@ -232,13 +254,34 @@
                 sent.append(
                     remote(
                         mid.at[(x + k) % 4], xi.at[k - 1],
-                        xs_s.at[i, k - 1], xs_r.at[i, k - 1], x_peer[k - 1],
+                        xs_s.at[i, 0, k - 1], xs_r.at[i, 0, k - 1], x_peer[k - 1],
                     )
                 )
         second.append(sent)
 
+    for i, (order, lo, n) in enumerate(CHUNKS):
+        xi, zi, mid = bufs[i]
+        for cp in second[i]:
+            take(cp)
+        if order == "xz":
+            acc = mid[t].astype(F32)
+            for k in range(7):
+                acc = acc + zi[k].astype(F32)
+        else:
+            acc = mid[x].astype(F32)
+            for k in range(3):
+                acc = acc + xi[k].astype(F32)
+        for j in range(n // 8):
+            sums[lo // 8 + j] = acc[8 * j : 8 * (j + 1), :]
+
+    ysent = []
+    for k in (4, 3, 5, 2, 6, 1, 7):
+        ysent.append(
+            remote(sums.at[(y + k) % 8], y_in.at[k - 1], ys_s.at[k - 1], ys_r.at[k - 1], y_peer[k - 1])
+        )
+
     for r in range(ROUNDS):
-        ret[r].wait_recv()
+        take(ret[r])
         v = slot_in[r].astype(F32)
         for b in range(2):
             own_sum[b] = own_sum[b] + v * (sblk[:, r : r + 1] == b).astype(F32)
@@ -249,54 +292,35 @@
     out2 = pltpu.make_async_copy(gnode_v, gnode_o.at[0], st.at[2])
     out2.start()
 
-    for i, (order, lo, n) in enumerate(CHUNKS):
-        xi, zi, mid = bufs[i]
-        for cp in second[i]:
-            cp.wait_recv()
-        if order == "xz":
-            acc = mid[t].astype(F32)
-            for k in range(7):
-                acc = acc + zi[k].astype(F32)
-        else:
-            acc = mid[x].astype(F32)
-            for k in range(3):
-                acc = acc + xi[k].astype(F32)
-        for j in range(n // 16):
-            sums[lo // 16 + j] = acc[16 * j : 16 * (j + 1), :].astype(BF16)
-
-    ysent = []
+    for cp in ysent:
+        take(cp)
+    acc = sums[y]
+    for k in range(7):
+        acc = acc + y_in[k]
+    fin[...] = acc
+    gsent = []
     for k in (4, 3, 5, 2, 6, 1, 7):
-        ysent.append(
-            remote(sums.at[(y + k) % 8], y_in.at[k - 1], ys_s.at[k - 1], ys_r.at[k - 1], y_peer[k - 1])
-        )
-    for cp in ysent:
-        cp.wait_recv()
-    acc = sums[y].astype(F32)
-    for k in range(7):
-        acc = acc + y_in[k].astype(F32)
-    fin[0] = acc[0:8, :]
-    fin[1] = acc[8:16, :]
-    slot = (t // 2, 2 * c + t % 2)
-    gsent = []
-    for i, dev in enumerate(g_peer):
-        half = c if i < 7 else 1 - c
-        gsent.append(remote(fin.at[half], gath.at[slot[0], slot[1]], ag_s.at[i], ag_r.at[i], dev))
-    mine = pltpu.make_async_copy(fin.at[c], gath.at[slot[0], slot[1]], st.at[3])
-    mine.start()
-    mine.wait()
+        gsent.append(remote(fin, gath.at[t], ag_s.at[k - 1], ag_r.at[k - 1], z_peer[k - 1]))
+    gath[t] = acc
     for cp in gsent:
-        cp.wait_recv()
-    for b in range(4):
-        wg_o[:, :, 128 * b : 128 * (b + 1)] = gath[:, b]
-
-    for r in range(ROUNDS):
-        ex[r].wait_send()
-        ret[r].wait_send()
-    for cp in core + first[0] + first[1] + second[0] + second[1] + ysent + gsent:
+        take(cp)
+    for m in range(4):
+        for b in range(2):
+            wg_o[m, :, 256 * b : 256 * (b + 1)] = gath[2 * m + b]
+
+    for cp in started:
         cp.wait_send()
     out0.wait()
     out1.wait()
     out2.wait()
+
+
+def place(*refs):
+    copies = [pltpu.make_async_copy(refs[i], refs[i + 4], refs[8].at[i]) for i in range(4)]
+    for cp in copies:
+        cp.start()
+    for cp in copies:
+        cp.wait()
 
 
 def per_device(
@@ -315,22 +339,23 @@
         vm(big, F32), vm(big, F32),
         vm(big, BF16), vm(big, BF16), vm(big, BF16), vm(big, BF16), vm(big, BF16),
         vm((4, 128, 512), BF16), vm((4, 128, 512), BF16),
-        vm((2, 4, 8, 128, 128), BF16), vm((4, 8, 128, 128), BF16), vm((4, 8, 128, 128), BF16),
+        vm((256, 512), BF16),
+        vm((2, 4, 8, 64, 256), BF16), vm((4, 8, 64, 256), BF16), vm((4, 8, 64, 256), BF16),
     ]
     for order, _, n in CHUNKS:
         if order == "xz":
-            scratch += [vm((3, 8, n, 128), BF16), vm((7, n, 128), BF16), vm((8, n, 128), BF16)]
+            scratch += [vm((3, 8, n, 256), BF16), vm((7, n, 256), BF16), vm((8, n, 256), BF16)]
         else:
-            scratch += [vm((3, n, 128), BF16), vm((7, 4, n, 128), BF16), vm((4, n, 128), BF16)]
+            scratch += [vm((3, n, 256), BF16), vm((7, 4, n, 256), BF16), vm((4, n, 256), BF16)]
     scratch += [
-        vm((8, 16, 128), BF16), vm((7, 16, 128), BF16), vm((2, 8, 128), F32), vm((4, 4, 8, 128), F32),
+        vm((8, 8, 256), F32), vm((7, 8, 256), F32), vm((8, 256), F32), vm((8, 8, 256), F32),
         vm((256, 512), BF16), vm(big, BF16), vm((256, 512), BF16),
         dma((12,)), dma((4,)), dma((4,)), dma((4,)), dma((4,)), dma((4,)), dma((4,)),
-        dma((2, 3)), dma((2, 3)), dma((2, 7)), dma((2, 7)), dma((7,)), dma((7,)),
-        dma((15,)), dma((15,)), dma((4,)),
+        dma((3, 2, 3)), dma((3, 2, 3)), dma((3, 7)), dma((3, 7)), dma((7,)), dma((7,)),
+        dma((7,)), dma((7,)), dma((3,)),
     ]
     hbm = pl.BlockSpec(memory_space=pl.ANY)
-    return pl.pallas_call(
+    results = pl.pallas_call(
         kernel,
         out_shape=(
             jax.ShapeDtypeStruct((1, 256, 512), BF16),
@@ -350,6 +375,14 @@
         edge_src.reshape(1, 512), edge_recv_block.reshape(1, 4),
         edge_recv_node.reshape(1, 512), send_blocks.reshape(1, 4),
     )
+    return pl.pallas_call(
+        place,
+        out_shape=tuple(jax.ShapeDtypeStruct(r.shape, r.dtype) for r in results),
+        in_specs=[hbm] * 4,
+        out_specs=(hbm,) * 4,
+        scratch_shapes=[dma((4,))],
+        name="place_results",
+    )(*results)
 
 
 def solution(mesh):

time: 67.9 us -> 94.4 us (1.39)
  Pallas kernels: 62.7 us -> 93.3 us
  local copies, waits for them, and re-layouts: 4.31 us -> 0 us
    pallas_call x0 -> x1, Pallas kernels: none -> 34.9 us  [per_device(): pl.pallas_call(place, out_shape=tuple((jax.ShapeDtypeStruct(r.shape, r.dt...]
    pallas_call x1, Pallas kernels: 62.7 us -> 58.4 us  [per_device(): pl.pallas_call(kernel, out_shape=(jax.ShapeDtypeStruct((1, 256, 512), BF1...]
    unnamed x10 -> x0, local copies, waits for them, and re-layouts: 4.31 us -> none
where the time goes in v2:
time: 94.4 us; the launch traced here: 93.9 us
  Pallas kernels  93.3 us (99%)
    pallas_call x1, Pallas kernels, per_device(): pl.pallas_call(kernel, out_shape=(jax.ShapeDtypeStruct((1, 256, 512), BF1...  58.4 us
    pallas_call x1, Pallas kernels, per_device(): pl.pallas_call(place, out_shape=tuple((jax.ShapeDtypeStruct(r.shape, r.dt...  34.9 us

profile of v2, /device:TPU:1, one launch (start us, length us, event | category | flops | bytes accessed | tf_op | source)
XLA Modules:
  0.0 93.9 jit_solution(17958811182608567909)
XLA Ops:
  0.6 58.4 %edge_update_backward.1 = (bf16[1,256,512]{2,1,0:T(8,128)(2,1)}, bf16[1,512,512]{2,1,0:T(8,128)(2,1)}, bf16[1,256,512]{2,1,0:T(8,128)(2,1)}, f32[4,8,512]{2,1,0:T(8,128)}) custom-call(bf16[1,256,512]{2,1,0:T(8,128)(2,1)} %node_h.1, bf16[1,512,512]{2,1,0:T(8,128)(2,1)} %edge_h.1, bf16[1,512,512]{2,1,0:T(8,128)(2,1)} %ge_h.1, bf16[1,256,512]{2,1,0:T(8,128)(2,1)} %ga_h.1, ...), custom_call_target="tpu_custom_call" | custom-call | tf_op jit(solution)/shard_map/edge_update_backward/pallas_call | solution.py:358
  59.1 34.9 %place_results.1 = (bf16[1,256,512]{2,1,0:T(8,128)(2,1)}, bf16[1,512,512]{2,1,0:T(8,128)(2,1)}, bf16[1,256,512]{2,1,0:T(8,128)(2,1)}, f32[4,8,512]{2,1,0:T(8,128)}) custom-call(bf16[1,256,512]{2,1,0:T(8,128)(2,1)} %get-tuple-element.8.refs_0_, bf16[1,512,512]{2,1,0:T(8,128)(2,1)} %get-tuple-element.9.refs_1_, ...), custom_call_target="tpu_custom_call" | custom-call | tf_op jit(solution)/shard_map/place_results/pallas_call | solution.py:378

commit v3 on v2

--- a/solution.py
+++ b/solution.py
@@ -30,8 +30,7 @@
     table, edge, ge, ga, we, ws, wr, wo, src, rnode, rblk, sblk,
     lent, oh, oht, rh, rht, pre, gmsg, srows, hid, msg, gproj, gpre, slot_out, slot_in,
     rsum, part, core_in, quart, x_in0, z_in0, mid0, x_in1, z_in1, mid1, x_in2, z_in2, mid2, sums, y_in, fin, gath,
-    agg_v, gedge_v, gnode_v,
-    ld, ex_s, ex_r, rt_s, rt_r, co_s, co_r, xs_s, xs_r, zs_s, zs_r, ys_s, ys_r, ag_s, ag_r, st,
+    ld, ex_s, ex_r, rt_s, rt_r, co_s, co_r, xs_s, xs_r, zs_s, zs_r, ys_s, ys_r, ag_s, ag_r,
 ):
     t = lax.axis_index("traj")
     d = lax.axis_index("dom")
@@ -215,14 +214,10 @@
     send_x(2, 0)
     send_x(2, 1)
 
-    agg_v[...] = mm(rht[...], msg[...]).astype(BF16)
-    out0 = pltpu.make_async_copy(agg_v, agg_o.at[0], st.at[0])
-    out0.start()
+    agg_o[0] = mm(rht[...], msg[...]).astype(BF16)
     for e in (0, 256):
         rows = slice(e, e + 256)
-        gedge_v[rows, :] = (ge[rows, :].astype(F32) + mm_nt(gpre[rows, :], we[...])).astype(BF16)
-    out1 = pltpu.make_async_copy(gedge_v, gedge_o.at[0], st.at[1])
-    out1.start()
+        gedge_o[0, rows, :] = (ge[rows, :].astype(F32) + mm_nt(gpre[rows, :], we[...])).astype(BF16)
     own_sum = [mm(oht[128 * b : 128 * (b + 1), :], gpre[...]) for b in range(2)]
     gn_recv = mm_nt(rsum[...], wr[...])
 
@@ -288,9 +283,7 @@
     for b in range(2):
         rows = slice(128 * b, 128 * (b + 1))
         gn = gn_recv[rows, :] + mm_nt(own_sum[b].astype(BF16), ws[...])
-        gnode_v[rows, :] = gn.astype(BF16)
-    out2 = pltpu.make_async_copy(gnode_v, gnode_o.at[0], st.at[2])
-    out2.start()
+        gnode_o[0, rows, :] = gn.astype(BF16)
 
     for cp in ysent:
         take(cp)
@@ -310,9 +303,6 @@
 
     for cp in started:
         cp.wait_send()
-    out0.wait()
-    out1.wait()
-    out2.wait()
 
 
 def place(*refs):
@@ -349,40 +339,38 @@
             scratch += [vm((3, n, 256), BF16), vm((7, 4, n, 256), BF16), vm((4, n, 256), BF16)]
     scratch += [
         vm((8, 8, 256), F32), vm((7, 8, 256), F32), vm((8, 256), F32), vm((8, 8, 256), F32),
-        vm((256, 512), BF16), vm(big, BF16), vm((256, 512), BF16),
         dma((12,)), dma((4,)), dma((4,)), dma((4,)), dma((4,)), dma((4,)), dma((4,)),
         dma((3, 2, 3)), dma((3, 2, 3)), dma((3, 7)), dma((3, 7)), dma((7,)), dma((7,)),
-        dma((7,)), dma((7,)), dma((3,)),
+        dma((7,)), dma((7,)),
     ]
-    hbm = pl.BlockSpec(memory_space=pl.ANY)
-    results = pl.pallas_call(
-        kernel,
-        out_shape=(
-            jax.ShapeDtypeStruct((1, 256, 512), BF16),
-            jax.ShapeDtypeStruct((1, 512, 512), BF16),
-            jax.ShapeDtypeStruct((1, 256, 512), BF16),
-            jax.ShapeDtypeStruct((4, 8, 512), F32),
-        ),
-        in_specs=[hbm] * 12,
-        out_specs=(hbm, hbm, hbm, pl.BlockSpec(memory_space=pltpu.VMEM)),
-        scratch_shapes=scratch,
-        compiler_params=pltpu.CompilerParams(
-            collective_id=0, has_side_effects=True, vmem_limit_bytes=56 << 20
-        ),
-        name="edge_update_backward",
-    )(
+    hbm = pl.BlockSpec(memory_space=pltpu.HBM)
+    vmem = pl.BlockSpec(memory_space=pltpu.VMEM)
+    operands = (
         node_lat, edge_lat, grad_edge, grad_agg, weight_edge, weight_send, weight_recv, weight_out,
         edge_src.reshape(1, 512), edge_recv_block.reshape(1, 4),
         edge_recv_node.reshape(1, 512), send_blocks.reshape(1, 4),
     )
+    results = pl.pallas_call(
+        kernel,
+        out_shape=(
+            vm((1, 256, 512), BF16), vm((1, 512, 512), BF16), vm((1, 256, 512), BF16), vm((4, 8, 512), F32),
+        ),
+        in_specs=[hbm] * 12,
+        out_specs=(vmem,) * 4,
+        scratch_shapes=scratch,
+        compiler_params=pltpu.CompilerParams(
+            collective_id=0, has_side_effects=True, vmem_limit_bytes=44 << 20
+        ),
+        name="edge_update_backward",
+    )(*(pltpu.with_memory_space_constraint(a, pltpu.HBM) for a in operands))
     return pl.pallas_call(
         place,
         out_shape=tuple(jax.ShapeDtypeStruct(r.shape, r.dtype) for r in results),
-        in_specs=[hbm] * 4,
+        in_specs=[pl.BlockSpec(memory_space=pl.ANY)] * 4,
         out_specs=(hbm,) * 4,
         scratch_shapes=[dma((4,))],
         name="place_results",
-    )(*results)
+    )(*(pltpu.with_memory_space_constraint(r, pltpu.VMEM) for r in results))
 
 
 def solution(mesh):

time: 94.4 us -> 59.8 us (0.63)
  Pallas kernels: 93.3 us -> 58.8 us
    pallas_call x1, Pallas kernels: 34.9 us -> 1.01 us  [per_device(): pl.pallas_call(place, out_shape=tuple((jax.ShapeDtypeStruct(r.shape, r.dt...]
where the time goes in v3:
time: 59.8 us; the launch traced here: 59.4 us
  Pallas kernels  58.8 us (98%)
  between operations  0.64 us (1%)
    pallas_call x1, Pallas kernels, per_device(): pl.pallas_call(kernel, out_shape=(vm((1, 256, 512), BF16), vm((1, 512, 51...  57.8 us

profile of v3, /device:TPU:1, one launch (start us, length us, event | category | flops | bytes accessed | tf_op | source)
XLA Modules:
  0.0 59.4 jit_solution(211131207280769012)
XLA Ops:
  0.6 57.8 %edge_update_backward.1 = (bf16[1,256,512]{2,1,0:T(8,128)(2,1)S(1)}, bf16[1,512,512]{2,1,0:T(8,128)(2,1)S(1)}, bf16[1,256,512]{2,1,0:T(8,128)(2,1)S(1)}, f32[4,8,512]{2,1,0:T(8,128)S(1)}) custom-call(bf16[1,256,512]{2,1,0:T(8,128)(2,1)} %node_h.1, bf16[1,512,512]{2,1,0:T(8,128)(2,1)} %edge_h.1, bf16[1,512,512]{2,1,0:T(8,128)(2,1)} %ge_h.1, ...), custom_call_target="tpu_custom_call" | custom-call | tf_op jit(solution)/shard_map/edge_update_backward/pallas_call | solution.py:353
  58.4 1.0 %place_results.1 = (bf16[1,256,512]{2,1,0:T(8,128)(2,1)}, bf16[1,512,512]{2,1,0:T(8,128)(2,1)}, bf16[1,256,512]{2,1,0:T(8,128)(2,1)}, f32[4,8,512]{2,1,0:T(8,128)}) custom-call(bf16[1,256,512]{2,1,0:T(8,128)(2,1)S(1)} %get-tuple-element.8.refs_0_, bf16[1,512,512]{2,1,0:T(8,128)(2,1)S(1)} %get-tuple-element.9.refs_1_, ...), custom_call_target="tpu_custom_call" | custom-call | tf_op jit(solution)/shard_map/place_results/pallas_call | solution.py:366

commit v4 on v3

--- a/solution.py
+++ b/solution.py
@@ -29,7 +29,7 @@
     agg_o, gedge_o, gnode_o, wg_o,
     table, edge, ge, ga, we, ws, wr, wo, src, rnode, rblk, sblk,
     lent, oh, oht, rh, rht, pre, gmsg, srows, hid, msg, gproj, gpre, slot_out, slot_in,
-    rsum, part, core_in, quart, x_in0, z_in0, mid0, x_in1, z_in1, mid1, x_in2, z_in2, mid2, sums, y_in, fin, gath,
+    rsum, part, core_in, quart, x_in0, z_in0, mid0, x_in1, z_in1, mid1, x_in2, z_in2, mid2, sums, y_in, fin, gath, edge_t, node_t, early, far0, mrg0, far2, mrg2,
     ld, ex_s, ex_r, rt_s, rt_r, co_s, co_r, xs_s, xs_r, zs_s, zs_r, ys_s, ys_r, ag_s, ag_r,
 ):
     t = lax.axis_index("traj")
@@ -55,6 +55,24 @@
 
     load(0, node_h.at[0], table.at[0:256])
     load(1, sblk_h, sblk)
+
+    bar = pltpu.get_barrier_semaphore()
+    greet = [partners[0]] + y_peer + x_peer + z_peer
+    for dev in greet:
+        pl.semaphore_signal(bar, inc=1, device_id=dev, device_id_type=MESH)
+
+    def remote(s, dst, ss, rs, dev):
+        cp = pltpu.make_async_remote_copy(
+            src_ref=s, dst_ref=dst, send_sem=ss, recv_sem=rs, device_id=dev, device_id_type=MESH
+        )
+        cp.start()
+        started.append(cp)
+        return cp
+
+    def take(cp):
+        cp.wait_recv()
+        taken.add(id(cp))
+
     load(2, src_h, src)
     load(3, rblk_h, rblk)
     load(4, rnode_h, rnode)
@@ -66,31 +84,13 @@
     load(10, ws_h, ws)
     load(11, wo_h, wo)
 
-    bar = pltpu.get_barrier_semaphore()
-    greet = [partners[0]] + y_peer + x_peer + z_peer
-    for dev in greet:
-        pl.semaphore_signal(bar, inc=1, device_id=dev, device_id_type=MESH)
-
-    def remote(s, dst, ss, rs, dev):
-        cp = pltpu.make_async_remote_copy(
-            src_ref=s, dst_ref=dst, send_sem=ss, recv_sem=rs, device_id=dev, device_id_type=MESH
-        )
-        cp.start()
-        started.append(cp)
-        return cp
-
-    def take(cp):
-        cp.wait_recv()
-        taken.add(id(cp))
-
     loads[0].wait()
     loads[1].wait()
-    for r in range(ROUNDS):
-        pick = jnp.broadcast_to(sblk[:, r : r + 1], (128, 512)) == 0
-        lent[r] = jnp.where(pick, table[0:128, :].astype(F32), table[128:256, :].astype(F32)).astype(BF16)
     pl.semaphore_wait(bar, len(greet))
     ex = {}
     for r in (3, 2, 1, 0):
+        pick = jnp.broadcast_to(sblk[:, r : r + 1], (128, 512)) == 0
+        lent[r] = jnp.where(pick, table[0:128, :].astype(F32), table[128:256, :].astype(F32)).astype(BF16)
         ex[r] = remote(
             lent.at[r], table.at[256 + 128 * r : 384 + 128 * r], ex_s.at[r], ex_r.at[r], partners[r]
         )
@@ -114,13 +114,19 @@
         gmsg[rows, :] = ge[rows, :].astype(F32) + mm(rh[rows, :], ga[...])
     for i in (10, 11):
         loads[i].wait()
-
-    for r in range(ROUNDS):
-        take(ex[r])
-
+    edge_t[...] = edge[...].T
+    node_t[...] = table[0:256, :].T
+    take(ex[0])
+    take(ex[1])
     for e in (0, 256):
         rows = slice(e, e + 256)
-        sr = mm(oh[rows, :], table[...]).astype(BF16)
+        early[rows, :] = mm(oh[rows, 0:512], table[0:512, :])
+    take(ex[2])
+    take(ex[3])
+
+    for e in (0, 256):
+        rows = slice(e, e + 256)
+        sr = (early[rows, :] + mm(oh[rows, 512:768], table[512:768, :])).astype(BF16)
         srows[rows, :] = sr
         p = pre[rows, :] + mm(sr, ws[...])
         sig = 1.0 / (1.0 + jnp.exp(-p))
@@ -146,13 +152,13 @@
 
     def grad(m):
         if m == 0:
-            gw = mm_tn(edge[...], gpre[...])
+            gw = mm(edge_t[...], gpre[...])
         elif m == 1:
+            gw = mm(node_t[...], rsum[...])
+        elif m == 2:
+            gw = mm_tn(hid[...], gproj[...])
+        else:
             gw = mm_tn(srows[...], gpre[...])
-        elif m == 2:
-            gw = mm_tn(table[0:256, :], rsum[...])
-        else:
-            gw = mm_tn(hid[...], gproj[...])
         gw = gw.reshape(4, 8, 2, 8, 512)
         for xx in range(4):
             for cc in range(2):
@@ -174,50 +180,80 @@
         z2 = slice(2 * m, 2 * m + 2)
         quart[:, z2] = (part[c, :, z2].astype(F32) + core_in[:, z2].astype(F32)).astype(BF16)
 
+    far, relays = {}, {0: (far0, mrg0), 2: (far2, mrg2)}
+
+    def put_x(i, slot, src, dst, k):
+        return remote(src, dst, xs_s.at[i, slot], xs_r.at[i, slot], x_peer[k - 1])
+
     def send_x(i, g):
         _, lo, n = CHUNKS[i]
-        zs = slice(4 * g, 4 * g + 4)
-        for k in (2, 1, 3):
-            first[i].append(
-                remote(
-                    quart.at[(x + k) % 4, zs, lo : lo + n], bufs[i][0].at[k - 1, zs],
-                    xs_s.at[i, g, k - 1], xs_r.at[i, g, k - 1], x_peer[k - 1],
-                )
-            )
-
-    def send_z(i):
+        zs, rs = slice(4 * g, 4 * g + 4), slice(lo, lo + n)
+        fwd, back = (1, 3) if g == 0 else (3, 1)
+        far[i, g] = put_x(i, g, quart.at[(x + 2) % 4, zs, rs], relays[i][0].at[g], fwd)
+        first[i].append(
+            put_x(i, 2 + g, quart.at[(x + back) % 4, zs, rs], bufs[i][0].at[1 - g, g], back)
+        )
+
+    def relay_x(i, g):
         _, lo, n = CHUNKS[i]
+        far_in, mrg = relays[i]
+        fwd = 1 if g == 0 else 3
+        take(far[i, g])
+        own = quart[(x + fwd) % 4, 4 * g : 4 * g + 4, lo : lo + n].astype(F32)
+        mrg[g] = (own + far_in[g].astype(F32)).astype(BF16)
+        first[i].append(put_x(i, 4 + g, mrg.at[g], bufs[i][0].at[g, g], fwd))
+
+    def copy_z(i, k):
+        _, lo, n = CHUNKS[i]
+        return pltpu.make_async_remote_copy(
+            src_ref=quart.at[:, (t + k) % 8, lo : lo + n], dst_ref=bufs[i][1].at[k - 1],
+            send_sem=zs_s.at[i, k - 1], recv_sem=zs_r.at[i, k - 1],
+            device_id=z_peer[k - 1], device_id_type=MESH,
+        )
+
+    def send_z(i, g):
         for k in (4, 3, 5, 2, 6, 1, 7):
-            first[i].append(
-                remote(
-                    quart.at[:, (t + k) % 8, lo : lo + n], bufs[i][1].at[k - 1],
-                    zs_s.at[i, k - 1], zs_r.at[i, k - 1], z_peer[k - 1],
-                )
-            )
+
+            @pl.when(((t + k) % 8) // 4 == g)
+            def _(k=k):
+                copy_z(i, k).start()
+
+        if g == 1:
+            for k in range(1, 8):
+                cp = copy_z(i, k)
+                started.append(cp)
+                first[i].append(cp)
 
     grad(0)
+    rsum[...] = mm(rht[...], gpre[...]).astype(BF16)
     grad(1)
-    rsum[...] = mm(rht[...], gpre[...]).astype(BF16)
     grad(2)
     merge(0)
     merge(1)
+    send_z(1, 0)
     send_x(0, 0)
+    send_x(2, 0)
     grad(3)
+    merge(2)
     for r in (3, 2, 1, 0):
         rows = slice(256 + 128 * r, 384 + 128 * r)
         slot_out[r] = mm(oht[rows, :], gpre[...]).astype(BF16)
+        if r == 2:
+            merge(3)
+            send_z(1, 1)
+            send_x(0, 1)
+            send_x(2, 1)
+    for r in (3, 2, 1, 0):
         ret[r] = remote(slot_out.at[r], slot_in.at[r], rt_s.at[r], rt_r.at[r], partners[r])
-    merge(2)
-    merge(3)
-    send_z(1)
-    send_x(0, 1)
-    send_x(2, 0)
-    send_x(2, 1)
 
     agg_o[0] = mm(rht[...], msg[...]).astype(BF16)
+    relay_x(0, 0)
+    relay_x(2, 0)
     for e in (0, 256):
         rows = slice(e, e + 256)
         gedge_o[0, rows, :] = (ge[rows, :].astype(F32) + mm_nt(gpre[rows, :], we[...])).astype(BF16)
+    relay_x(0, 1)
+    relay_x(2, 1)
     own_sum = [mm(oht[128 * b : 128 * (b + 1), :], gpre[...]) for b in range(2)]
     gn_recv = mm_nt(rsum[...], wr[...])
 
@@ -230,8 +266,8 @@
         sent = []
         if order == "xz":
             acc = quart[x, :, rs].astype(F32)
-            for k in range(3):
-                acc = acc + xi[k].astype(F32)
+            for k in range(2):
+                acc = acc + xi[k].astype(F32).reshape(8, n, 256)
             mid[...] = acc.astype(BF16)
             for k in (4, 3, 5, 2, 6, 1, 7):
                 sent.append(
@@ -249,7 +285,7 @@
                 sent.append(
                     remote(
                         mid.at[(x + k) % 4], xi.at[k - 1],
-                        xs_s.at[i, 0, k - 1], xs_r.at[i, 0, k - 1], x_peer[k - 1],
+                        xs_s.at[i, k - 1], xs_r.at[i, k - 1], x_peer[k - 1],
                     )
                 )
         second.append(sent)
@@ -267,7 +303,7 @@
             for k in range(3):
                 acc = acc + xi[k].astype(F32)
         for j in range(n // 8):
-            sums[lo // 8 + j] = acc[8 * j : 8 * (j + 1), :]
+            sums[lo // 8 + j] = acc[8 * j : 8 * (j + 1), :].astype(BF16)
 
     ysent = []
     for k in (4, 3, 5, 2, 6, 1, 7):
@@ -285,11 +321,14 @@
         gn = gn_recv[rows, :] + mm_nt(own_sum[b].astype(BF16), ws[...])
         gnode_o[0, rows, :] = gn.astype(BF16)
 
+    for cp in started[:-7]:
+        cp.wait_send()
     for cp in ysent:
         take(cp)
-    acc = sums[y]
+    acc = sums[y].astype(F32)
     for k in range(7):
-        acc = acc + y_in[k]
+        acc = acc + y_in[k].astype(F32)
+    acc = acc.astype(BF16)
     fin[...] = acc
     gsent = []
     for k in (4, 3, 5, 2, 6, 1, 7):
@@ -299,9 +338,9 @@
         take(cp)
     for m in range(4):
         for b in range(2):
-            wg_o[m, :, 256 * b : 256 * (b + 1)] = gath[2 * m + b]
-
-    for cp in started:
+            wg_o[(0, 2, 3, 1)[m], :, 256 * b : 256 * (b + 1)] = gath[2 * m + b].astype(F32)
+
+    for cp in ysent + gsent:
         cp.wait_send()
 
 
@@ -334,13 +373,15 @@
     ]
     for order, _, n in CHUNKS:
         if order == "xz":
-            scratch += [vm((3, 8, n, 256), BF16), vm((7, n, 256), BF16), vm((8, n, 256), BF16)]
+            scratch += [vm((2, 2, 4, n, 256), BF16), vm((7, n, 256), BF16), vm((8, n, 256), BF16)]
         else:
             scratch += [vm((3, n, 256), BF16), vm((7, 4, n, 256), BF16), vm((4, n, 256), BF16)]
     scratch += [
-        vm((8, 8, 256), F32), vm((7, 8, 256), F32), vm((8, 256), F32), vm((8, 8, 256), F32),
+        vm((8, 8, 256), BF16), vm((7, 8, 256), BF16), vm((8, 256), BF16), vm((8, 8, 256), BF16),
+        vm(big, BF16), vm((512, 256), BF16), vm(big, F32),
+        *[vm((2, 4, CHUNKS[i][2], 256), BF16) for i in (0, 0, 2, 2)],
         dma((12,)), dma((4,)), dma((4,)), dma((4,)), dma((4,)), dma((4,)), dma((4,)),
-        dma((3, 2, 3)), dma((3, 2, 3)), dma((3, 7)), dma((3, 7)), dma((7,)), dma((7,)),
+        dma((3, 6)), dma((3, 6)), dma((3, 7)), dma((3, 7)), dma((7,)), dma((7,)),
         dma((7,)), dma((7,)),
     ]
     hbm = pl.BlockSpec(memory_space=pltpu.HBM)

time: 59.8 us -> 59.2 us (0.990)
  the two profiles are of different devices: /device:TPU:1 before, /device:TPU:2 now
where the time goes in v4:
time: 59.2 us; the launch traced here: 59.1 us
  Pallas kernels  58.5 us (99%)
  between operations  0.64 us (1%)
    pallas_call x1, Pallas kernels, per_device(): pl.pallas_call(kernel, out_shape=(vm((1, 256, 512), BF16), vm((1, 512, 51...  57.4 us

profile of v4, /device:TPU:2, one launch (start us, length us, event | category | flops | bytes accessed | tf_op | source)
XLA Modules:
  0.0 59.1 jit_solution(6309828538496669973)
XLA Ops:
  0.6 57.4 %edge_update_backward.1 = (bf16[1,256,512]{2,1,0:T(8,128)(2,1)S(1)}, bf16[1,512,512]{2,1,0:T(8,128)(2,1)S(1)}, bf16[1,256,512]{2,1,0:T(8,128)(2,1)S(1)}, f32[4,8,512]{2,1,0:T(8,128)S(1)}) custom-call(bf16[1,256,512]{2,1,0:T(8,128)(2,1)} %node_h.1, bf16[1,512,512]{2,1,0:T(8,128)(2,1)} %edge_h.1, bf16[1,512,512]{2,1,0:T(8,128)(2,1)} %ge_h.1, ...), custom_call_target="tpu_custom_call" | custom-call | tf_op jit(solution)/shard_map/edge_update_backward/pallas_call | solution.py:394
  58.1 1.0 %place_results.1 = (bf16[1,256,512]{2,1,0:T(8,128)(2,1)}, bf16[1,512,512]{2,1,0:T(8,128)(2,1)}, bf16[1,256,512]{2,1,0:T(8,128)(2,1)}, f32[4,8,512]{2,1,0:T(8,128)}) custom-call(bf16[1,256,512]{2,1,0:T(8,128)(2,1)S(1)} %get-tuple-element.8.refs_0_, bf16[1,512,512]{2,1,0:T(8,128)(2,1)S(1)} %get-tuple-element.9.refs_1_, ...), custom_call_target="tpu_custom_call" | custom-call | tf_op jit(solution)/shard_map/place_results/pallas_call | solution.py:407

commit v5 on v4

--- a/solution.py
+++ b/solution.py
@@ -73,6 +73,17 @@
         cp.wait_recv()
         taken.add(id(cp))
 
+    loads[0].wait()
+    loads[1].wait()
+    pl.semaphore_wait(bar, len(greet))
+    ex = {}
+    for r in (3, 2, 1, 0):
+        pick = jnp.broadcast_to(sblk[:, r : r + 1], (128, 512)) == 0
+        lent[r] = jnp.where(pick, table[0:128, :].astype(F32), table[128:256, :].astype(F32)).astype(BF16)
+        ex[r] = remote(
+            lent.at[r], table.at[256 + 128 * r : 384 + 128 * r], ex_s.at[r], ex_r.at[r], partners[r]
+        )
+
     load(2, src_h, src)
     load(3, rblk_h, rblk)
     load(4, rnode_h, rnode)
@@ -83,17 +94,6 @@
     load(9, ge_h.at[0], ge)
     load(10, ws_h, ws)
     load(11, wo_h, wo)
-
-    loads[0].wait()
-    loads[1].wait()
-    pl.semaphore_wait(bar, len(greet))
-    ex = {}
-    for r in (3, 2, 1, 0):
-        pick = jnp.broadcast_to(sblk[:, r : r + 1], (128, 512)) == 0
-        lent[r] = jnp.where(pick, table[0:128, :].astype(F32), table[128:256, :].astype(F32)).astype(BF16)
-        ex[r] = remote(
-            lent.at[r], table.at[256 + 128 * r : 384 + 128 * r], ex_s.at[r], ex_r.at[r], partners[r]
-        )
 
     for i in (2, 3, 4):
         loads[i].wait()
@@ -124,8 +124,8 @@
     take(ex[2])
     take(ex[3])
 
-    for e in (0, 256):
-        rows = slice(e, e + 256)
+    for e in (0,):
+        rows = slice(e, e + 512)
         sr = (early[rows, :] + mm(oh[rows, 512:768], table[512:768, :])).astype(BF16)
         srows[rows, :] = sr
         p = pre[rows, :] + mm(sr, ws[...])
@@ -257,8 +257,9 @@
     own_sum = [mm(oht[128 * b : 128 * (b + 1), :], gpre[...]) for b in range(2)]
     gn_recv = mm_nt(rsum[...], wr[...])
 
-    second = []
-    for i, (order, lo, n) in enumerate(CHUNKS):
+    second = {}
+    for i in (0, 2, 1):
+        order, lo, n = CHUNKS[i]
         xi, zi, mid = bufs[i]
         rs = slice(lo, lo + n)
         for cp in first[i]:
@@ -288,9 +289,13 @@
                         xs_s.at[i, k - 1], xs_r.at[i, k - 1], x_peer[k - 1],
                     )
                 )
-        second.append(sent)
-
-    for i, (order, lo, n) in enumerate(CHUNKS):
+        second[i] = sent
+    settled = [ex[r] for r in range(ROUNDS)] + core + list(far.values())
+    for cp in settled + first[0] + first[1] + first[2]:
+        cp.wait_send()
+
+    for i in (0, 1, 2):
+        order, lo, n = CHUNKS[i]
         xi, zi, mid = bufs[i]
         for cp in second[i]:
             take(cp)
@@ -311,18 +316,6 @@
             remote(sums.at[(y + k) % 8], y_in.at[k - 1], ys_s.at[k - 1], ys_r.at[k - 1], y_peer[k - 1])
         )
 
-    for r in range(ROUNDS):
-        take(ret[r])
-        v = slot_in[r].astype(F32)
-        for b in range(2):
-            own_sum[b] = own_sum[b] + v * (sblk[:, r : r + 1] == b).astype(F32)
-    for b in range(2):
-        rows = slice(128 * b, 128 * (b + 1))
-        gn = gn_recv[rows, :] + mm_nt(own_sum[b].astype(BF16), ws[...])
-        gnode_o[0, rows, :] = gn.astype(BF16)
-
-    for cp in started[:-7]:
-        cp.wait_send()
     for cp in ysent:
         take(cp)
     acc = sums[y].astype(F32)
@@ -334,6 +327,18 @@
     for k in (4, 3, 5, 2, 6, 1, 7):
         gsent.append(remote(fin, gath.at[t], ag_s.at[k - 1], ag_r.at[k - 1], z_peer[k - 1]))
     gath[t] = acc
+    for r in range(ROUNDS):
+        take(ret[r])
+        v = slot_in[r].astype(F32)
+        for b in range(2):
+            own_sum[b] = own_sum[b] + v * (sblk[:, r : r + 1] == b).astype(F32)
+    for b in range(2):
+        rows = slice(128 * b, 128 * (b + 1))
+        gn = gn_recv[rows, :] + mm_nt(own_sum[b].astype(BF16), ws[...])
+        gnode_o[0, rows, :] = gn.astype(BF16)
+
+    for cp in list(ret.values()) + second[0] + second[1] + second[2]:
+        cp.wait_send()
     for cp in gsent:
         take(cp)
     for m in range(4):

time: 59.2 us -> 58.7 us (level)
  Pallas kernels: 58.5 us -> 57.9 us
where the time goes in v5:
time: 58.7 us; the launch traced here: 58.6 us
  Pallas kernels  57.9 us (99%)
  between operations  0.64 us (1%)
    pallas_call x1, Pallas kernels, per_device(): pl.pallas_call(kernel, out_shape=(vm((1, 256, 512), BF16), vm((1, 512, 51...  56.9 us

profile of v5, /device:TPU:2, one launch (start us, length us, event | category | flops | bytes accessed | tf_op | source)
XLA Modules:
  0.0 58.6 jit_solution(1830383396389899986)
XLA Ops:
  0.6 56.9 %edge_update_backward.1 = (bf16[1,256,512]{2,1,0:T(8,128)(2,1)S(1)}, bf16[1,512,512]{2,1,0:T(8,128)(2,1)S(1)}, bf16[1,256,512]{2,1,0:T(8,128)(2,1)S(1)}, f32[4,8,512]{2,1,0:T(8,128)S(1)}) custom-call(bf16[1,256,512]{2,1,0:T(8,128)(2,1)} %node_h.1, bf16[1,512,512]{2,1,0:T(8,128)(2,1)} %edge_h.1, bf16[1,512,512]{2,1,0:T(8,128)(2,1)} %ge_h.1, ...), custom_call_target="tpu_custom_call" | custom-call | tf_op jit(solution)/shard_map/edge_update_backward/pallas_call | solution.py:399
  57.6 1.0 %place_results.1 = (bf16[1,256,512]{2,1,0:T(8,128)(2,1)}, bf16[1,512,512]{2,1,0:T(8,128)(2,1)}, bf16[1,256,512]{2,1,0:T(8,128)(2,1)}, f32[4,8,512]{2,1,0:T(8,128)}) custom-call(bf16[1,256,512]{2,1,0:T(8,128)(2,1)S(1)} %get-tuple-element.8.refs_0_, bf16[1,512,512]{2,1,0:T(8,128)(2,1)S(1)} %get-tuple-element.9.refs_1_, ...), custom_call_target="tpu_custom_call" | custom-call | tf_op jit(solution)/shard_map/place_results/pallas_call | solution.py:412
